TPU v7x, 256 devices: a whole 4x4x8 slice. The times are simulated.
256 devices in a mesh: ia: 4 (over y), ja: 8 (over x, core), ka: 8 (over z).
Axes of the slice: x: 4, y: 4, z: 8, core: 2. Of those that a mesh axis runs over, the one named last changes fastest.
Arguments:
- observed: bfloat16 [4, 8, 40, 128, 32, 128], P('ia', 'ja', 'ka'), may hold values from -6 to 6
- weights: bfloat16 [4, 8, 40, 128, 32, 128], P('ia', 'ja', 'ka'), may hold values from 0 to 4, as said below
- coords: int32 [4, 8, 40, 3], P('ia', 'ja', 'ka'), may hold values from 0 to 31, as said below
- counts: int32 [4, 8, 8], P('ia', 'ja', 'ka'), may hold values from 0 to 5, as said below
- factor_rows: bfloat16 [64, 4096], P(None, ('ia', 'ja', 'ka')), may hold values from -0.75 to 0.75
- factor_cols: bfloat16 [64, 4096], P(None, ('ja', 'ka')), may hold values from -0.75 to 0.75
- factor_depth: bfloat16 [64, 1024], replicated, may hold values from -0.75 to 0.75
- core_tensor: bfloat16 [64, 64, 64], replicated, may hold values from -6 to 6
Outputs:
- rows_gradient: float32 [64, 4096], P(None, ('ia', 'ja', 'ka'))
- cols_gradient: float32 [64, 4096], P(None, ('ja', 'ka'))
- depth_gradient: float32 [64, 1024], P(None, 'ka')
- core_gradient: float32 [64, 64, 64], replicated
Inputs may be any that keep to these rules, and one draw needn't show every extreme that they name: counts[a, b, c] is the number of live slots of the device at index a of ia, b of ja, c of ka; the busiest devices hold 5. coords[a, b, c * 5 + s] = (p, q, t) with a * 8 <= p < (a + 1) * 8, b * 4 <= q < (b + 1) * 4, c * 4 <= t < (c + 1) * 4; the 5 slots of one device name distinct blocks. `weights`: zero at unobserved entries, positive at observed ones.
All inputs are finite; a program needn't handle non-finite values.
Results may differ from a plain program's by a relative error of at most 0.0012.
Values may be sent and summed in bfloat16 or wider, within the bound.
A program may use at most 64 MiB of HBM per device.

v0:
```python
import jax
import jax.numpy as jnp
from jax import lax
from jax.sharding import PartitionSpec as P

resid_scale = 1.0 / 64.0


def block_terms(observed_block, weight_block, row_factor, col_factor, depth_factor, core_tensor):
    rank_width, block_rows = row_factor.shape
    block_cols = col_factor.shape[1]
    slab_depth = depth_factor.shape[1]
    core_flat = core_tensor.reshape(rank_width * rank_width, rank_width)
    first_cube = jnp.dot(core_flat, depth_factor, preferred_element_type=jnp.float32).astype(
        jnp.bfloat16
    )
    first_cube = first_cube.reshape(rank_width, rank_width, slab_depth)
    second_cube = jnp.einsum(
        "rsk,sj->rkj", first_cube, col_factor, preferred_element_type=jnp.float32
    ).astype(jnp.bfloat16)
    second_flat = second_cube.reshape(rank_width, slab_depth * block_cols)
    model_block = lax.dot_general(
        row_factor, second_flat, (((0,), (0,)), ((), ())), preferred_element_type=jnp.float32
    )
    weight_flat = weight_block.reshape(block_rows, slab_depth * block_cols).astype(jnp.float32)
    data_flat = observed_block.reshape(block_rows, slab_depth * block_cols).astype(jnp.float32)
    residual = (weight_flat * (model_block - data_flat) * resid_scale).astype(jnp.bfloat16)
    row_term = lax.dot_general(
        second_flat, residual, (((1,), (1,)), ((), ())), preferred_element_type=jnp.float32
    )
    first_back = jnp.dot(row_factor, residual, preferred_element_type=jnp.float32).astype(
        jnp.bfloat16
    )
    back_cube = first_back.reshape(rank_width, slab_depth, block_cols)
    col_term = jnp.einsum("rsk,rkj->sj", first_cube, back_cube, preferred_element_type=jnp.float32)
    second_back = jnp.einsum(
        "sj,rkj->rsk", col_factor, back_cube, preferred_element_type=jnp.float32
    ).astype(jnp.bfloat16)
    back_flat = second_back.reshape(rank_width * rank_width, slab_depth)
    depth_term = lax.dot_general(
        core_flat, back_flat, (((0,), (0,)), ((), ())), preferred_element_type=jnp.float32
    )
    core_term = lax.dot_general(
        back_flat, depth_factor, (((1,), (1,)), ((), ())), preferred_element_type=jnp.float32
    )
    return (row_term, col_term, depth_term, core_term.reshape(rank_width, rank_width, rank_width))


def add_columns(table, piece, start_col):
    width = piece.shape[1]
    return lax.dynamic_update_slice_in_dim(
        table, lax.dynamic_slice_in_dim(table, start_col, width, 1) + piece, start_col, 1
    )


def accumulate_blocks(
    live_count,
    data_slots,
    weight_slots,
    coord_slots,
    row_table,
    col_table,
    factor_depth,
    core_tensor,
    row_base,
    col_base,
):
    rank_width = core_tensor.shape[0]
    block_rows = data_slots.shape[1]
    slab_depth = data_slots.shape[2]
    block_cols = data_slots.shape[3]
    start_sums = (
        jnp.zeros((rank_width, row_table.shape[1]), jnp.float32),
        jnp.zeros((rank_width, col_table.shape[1]), jnp.float32),
        jnp.zeros((rank_width, factor_depth.shape[1]), jnp.float32),
        jnp.zeros((rank_width, rank_width, rank_width), jnp.float32),
    )

    def add_slot(slot_index, running):
        rows_sum, cols_sum, depth_sum, core_sum = running
        position = coord_slots[slot_index]
        row_start = (position[0] - row_base) * block_rows
        col_start = (position[1] - col_base) * block_cols
        depth_start = position[2] * slab_depth
        row_factor = lax.dynamic_slice_in_dim(row_table, row_start, block_rows, 1)
        col_factor = lax.dynamic_slice_in_dim(col_table, col_start, block_cols, 1)
        depth_factor = lax.dynamic_slice_in_dim(factor_depth, depth_start, slab_depth, 1)
        block_sums = block_terms(
            data_slots[slot_index],
            weight_slots[slot_index],
            row_factor,
            col_factor,
            depth_factor,
            core_tensor,
        )
        rows_sum = add_columns(rows_sum, block_sums[0], row_start)
        cols_sum = add_columns(cols_sum, block_sums[1], col_start)
        depth_sum = add_columns(depth_sum, block_sums[2], depth_start)
        return (rows_sum, cols_sum, depth_sum, core_sum + block_sums[3])

    return lax.fori_loop(0, live_count, add_slot, start_sums)


def on_device(
    observed, weights, coords, counts, factor_rows, factor_cols, factor_depth, core_tensor
):
    slot_count = observed.shape[2]
    data_slots = observed.reshape(observed.shape[2:])
    weight_slots = weights.reshape(weights.shape[2:])
    coord_slots = coords.reshape(slot_count, 3)
    own_count = counts.reshape(())
    row_table = lax.all_gather(factor_rows, ("ja", "ka"), axis=1, tiled=True)
    col_table = lax.all_gather(factor_cols, "ka", axis=1, tiled=True)
    row_base = lax.axis_index("ia") * (row_table.shape[1] // observed.shape[3])
    col_base = lax.axis_index("ja") * (col_table.shape[1] // observed.shape[5])
    rows_sum, cols_sum, depth_sum, core_sum = accumulate_blocks(
        own_count,
        data_slots,
        weight_slots,
        coord_slots,
        row_table,
        col_table,
        factor_depth,
        core_tensor,
        row_base,
        col_base,
    )
    rows_gradient = lax.psum_scatter(rows_sum, ("ja", "ka"), scatter_dimension=1, tiled=True)
    cols_whole = lax.psum(cols_sum, "ia")
    depth_whole = lax.psum(depth_sum, ("ia", "ja"))
    cols_gradient, depth_gradient = (
        lax.psum_scatter(cols_whole, "ka", scatter_dimension=1, tiled=True),
        lax.psum_scatter(depth_whole, "ka", scatter_dimension=1, tiled=True),
    )
    core_gradient = lax.psum(core_sum, ("ia", "ja", "ka"))
    return (rows_gradient, cols_gradient, depth_gradient, core_gradient)


def solution(mesh):
    in_specs = (
        P("ia", "ja", "ka", None, None, None),
        P("ia", "ja", "ka", None, None, None),
        P("ia", "ja", "ka", None),
        P("ia", "ja", "ka"),
        P(None, ("ia", "ja", "ka")),
        P(None, ("ja", "ka")),
        P(),
        P(),
    )
    out_specs = (P(None, ("ia", "ja", "ka")), P(None, ("ja", "ka")), P(None, "ka"), P())
    return jax.shard_map(
        on_device, mesh=mesh, in_specs=in_specs, out_specs=out_specs, check_vma=False
    )
```

profile of v0, /device:TPU:2, one launch (start us, length us, event | category | flops | bytes accessed | tf_op | source)
XLA Modules:
  0.0 616.1 jit_solution(5447334796632463020)
XLA Ops:
  8.0 46.2 %all_gather.7 = bf16[64,1024]{0,1:T(8,128)(2,1)S(1)} all-gather(bf16[64,16]{0,1:T(8,128)(2,1)} %param.14), channel_id=1, replica_groups=mesh['ia'=4,'ja'=8,'ka'=8] {'ja','ka'}, dimensions={1}, use_global_device_ids=true | all-gather | bytes 133120 | tf_op jit(solution)/shard_map/all_gather | solution.py:112
  54.3 1.1 copy.25
  55.5 0.8 copy.23
  56.3 24.6 %all_gather.6 = bf16[64,512]{0,1:T(8,128)(2,1)S(1)} all-gather(bf16[64,64]{0,1:T(8,128)(2,1)S(1)} %copy.23), channel_id=1, replica_groups=mesh['ia'=4,'ja'=8,'ka'=8] {'ka'}, dimensions={1}, use_global_device_ids=true | all-gather | bytes 73728 | tf_op jit(solution)/shard_map/all_gather | solution.py:113
  81.0 0.7 copy.56
  81.7 1.6 broadcast_in_dim.7
  83.3 70.1 %while.16 = (s32[]{:T(128)}, f32[64,1024]{1,0:T(8,128)S(1)}, f32[64,512]{1,0:T(8,128)S(1)}, f32[64,1024]{0,1:T(8,128)S(1)}, f32[64,64,64]{2,1,0:T(8,128)}, /*ind...) while((s32[]{:T(128)}, f32[64,1024]{1,0:T(8,128)S(1)}, ...), condition=%wide.region_1.0_spmd, body=%wide.region_0.0_spmd.sunk | while | flops 356534272 | bytes 34849308 | solution.py:101
  84.1 0.6 fusion.87
  85.3 0.4 fusion.88
  85.7 0.6 reshape.62
  88.0 2.1 dynamic-slice_convert_fusion.3
  90.1 2.7 fusion.89
  93.5 0.9 copy-done.1
  94.4 0.7 convolution_add_fusion.3
  95.4 1.0 copy-done.2
  96.7 0.5 fusion.90
  98.0 0.6 fusion.87
  99.2 0.4 fusion.88
  99.6 0.6 reshape.62
  101.9 2.1 dynamic-slice_convert_fusion.3
  104.0 2.7 fusion.89
  107.4 0.9 copy-done.1
  108.3 0.7 convolution_add_fusion.3
  109.3 1.0 copy-done.2
  110.6 0.5 fusion.90
  111.8 0.6 fusion.87
  113.0 0.4 fusion.88
  113.5 0.6 reshape.62
  115.7 2.1 dynamic-slice_convert_fusion.3
  117.9 2.7 fusion.89
  121.3 0.9 copy-done.1
  122.2 0.7 convolution_add_fusion.3
  123.2 1.0 copy-done.2
  124.5 0.5 fusion.90
  125.7 0.6 fusion.87
  126.9 0.4 fusion.88
  127.4 0.6 reshape.62
  129.6 2.1 dynamic-slice_convert_fusion.3
  131.8 2.7 fusion.89
  135.2 0.9 copy-done.1
  136.0 0.7 convolution_add_fusion.3
  137.1 1.0 copy-done.2
  138.3 0.5 fusion.90
  139.6 0.6 fusion.87
  140.8 0.4 fusion.88
  141.2 0.6 reshape.62
  143.5 2.1 dynamic-slice_convert_fusion.3
  145.6 2.7 fusion.89
  149.0 0.9 copy-done.1
  149.9 0.7 convolution_add_fusion.3
  150.9 1.0 copy-done.2
  152.2 0.5 fusion.90
  153.4 1.0 copy.28
  154.5 0.8 copy.31
  155.4 0.9 copy.29
  156.4 0.7 all-reduce.4.cloned.1.call-update
  157.1 0.6 dynamic-slice
  158.3 179.5 %all-reduce.6.cloned.1.call-done = f32[64,1024]{0,1:T(8,128)} async-done(((f32[64,1024]{0,1:T(8,128)}), f32[64,1024]{0,1:T(8,128)}) %all-reduce.6.cloned.1.call-update) | async-done | bytes 262160
  337.8 1.3 constant_dynamic-slice_fusion.1
  339.1 0.8 copy.32
  340.0 17.6 %psum.24 = f32[64,64]{1,0:T(8,128)} all-reduce(f32[64,64]{1,0:T(8,128)S(1)} %copy.32), channel_id=1, replica_groups=mesh['ia'=4,'ja'=8,'ka'=8] {'ia'}, use_global_device_ids=true, to_apply=%region_3.0 | all-reduce | flops 4096 | bytes 32768 | tf_op jit(solution)/shard_map/psum | solution.py:129
  357.6 119.0 %psum.25 = f32[64,128]{1,0:T(8,128)} all-reduce(f32[64,128]{1,0:T(8,128)} %reduce-scatter.5.cloned.1.call-done), channel_id=1, replica_groups=mesh['ia'=4,'ja'=8,'ka'=8] {'ia','ja'}, use_global_device_ids=true, to_apply=%region_5.0 | all-reduce | flops 8192 | bytes 65536 | tf_op jit(solution)/shard_map/psum | solution.py:130
  476.6 129.0 %all-reduce.4.cloned.1.call-done = f32[64,64,64]{2,1,0:T(8,128)} async-done(((f32[64,64,64]{2,1,0:T(8,128)}), f32[64,64,64]{2,1,0:T(8,128)}) %all-reduce.4.cloned.1.call-update) | async-done | bytes 1048592 | tf_op jit(solution)/shard_map/psum | solution.py:135
  605.5 3.2 copy.91
  (63 shorter events, 9.4 us)
Async XLA Ops:
  8.0 329.8 %all-reduce.6.cloned.1.call-start = ((), (), s32[]{:S(2)}) async-start(), calls=%async_computation.5 | async-start | bytes 1048576
  54.2 29.1 %copy-start = (bf16[64,64,64]{2,1,0:T(8,128)(2,1)S(1)}, bf16[64,64,64]{2,1,0:T(8,128)(2,1)}, u32[]{:S(2)}) copy-start(bf16[64,64,64]{2,1,0:T(8,128)(2,1)} %param.17) | copy-start | bytes 1572868
  92.8 1.6 copy-start.1
  95.1 1.3 copy-start.2
  106.7 1.6 copy-start.1
  109.0 1.3 copy-start.2
  120.6 1.6 copy-start.1
  122.8 1.3 copy-start.2
  134.4 1.6 copy-start.1
  136.7 1.3 copy-start.2
  148.3 1.6 copy-start.1
  150.6 1.3 copy-start.2
  154.4 2.7 copy-start.3
  154.4 184.7 %reduce-scatter.7.cloned.1.call-start = ((), (), s32[]{:S(2)}) async-start(), calls=%async_computation.4 | async-start | bytes 294912
  155.3 202.3 %reduce-scatter.5.cloned.1.call-start = ((), (), s32[]{:S(2)}) async-start(), calls=%async_computation.3 | async-start | bytes 294912 | tf_op jit(solution)/shard_map/reduce_scatter | solution.py:133
  156.3 449.2 %all-reduce.4.cloned.1.call-start = ((), (), s32[]{:S(2)}) async-start(), calls=%async_computation.2 | async-start | bytes 4194304 | tf_op jit(solution)/shard_map/psum | solution.py:135
Sparse Core Ops, SparseCore 0:
  154.6 183.2 all-reduce.5
  343.8 261.6 all-reduce.3
Sparse Core Ops, SparseCore 1:
  157.4 36.2 reduce-scatter.6
  196.0 35.9 reduce-scatter.4
where the time goes:
time: 617 us; the launch traced here: 616 us
  waiting for transfers between devices  309 us (50%)
  blocking collectives  207 us (34%)
  matrix products  29.4 us (5%)
  local copies, waits for them, and re-layouts  29.1 us (5%)
  between operations  16.2 us (3%)
  loops' own time  14 us (2%)
  other arithmetic  10.7 us (2%)
    unnamed x6, waiting for transfers between devices  180 us
    psum x1, waiting for transfers between devices, on_device(): core_gradient = lax.psum(core_sum, ('ia', 'ja', 'ka'))  129 us
    psum x1, blocking collectives, on_device(): depth_whole = lax.psum(depth_sum, ('ia', 'ja'))  119 us
    all_gather x1, blocking collectives, on_device(): row_table = lax.all_gather(factor_rows, ('ja', 'ka'), axis=1, tiled=True)  46.2 us
    all_gather x1, blocking collectives, on_device(): col_table = lax.all_gather(factor_cols, 'ka', axis=1, tiled=True)  24.6 us
    psum x1, blocking collectives, on_device(): cols_whole = lax.psum(cols_sum, 'ia')  17.6 us
    another operation x1, loops' own time, accumulate_blocks(): return lax.fori_loop(0, live_count, add_slot, start_sums)  14 us
    dot_general x5, matrix products, block_terms(): lax.dot_general(row_factor, second_flat, (((0,), (0,)), ((), ())), prefer...  13.4 us
  transfers between devices with their start and end apart: 4, of which 2 were waited for; matrix products, arithmetic and copies ran while one was open for 1% of the time, Pallas kernels for 0%

commit v1 on v0

--- a/solution.py
+++ b/solution.py
@@ -132,7 +132,8 @@
         lax.psum_scatter(cols_whole, "ka", scatter_dimension=1, tiled=True),
         lax.psum_scatter(depth_whole, "ka", scatter_dimension=1, tiled=True),
     )
-    core_gradient = lax.psum(core_sum, ("ia", "ja", "ka"))
+    one_axis = lax.psum(core_sum, ("ja", "ka"))
+    core_gradient = lax.psum(one_axis, "ia")
     return (rows_gradient, cols_gradient, depth_gradient, core_gradient)
 
 

time: 617 us -> 502 us (0.81)
  waiting for transfers between devices: 309 us -> 190 us
    psum x1, waiting for transfers between devices: 129 us -> 0.01 us  [on_device(): core_gradient = lax.psum(one_axis, 'ia')]
    unnamed x6, waiting for transfers between devices: 180 us -> 190 us
  transfers between devices with their start and end apart: 4 -> 4, of which waited for: 2 -> 1; matrix products, arithmetic and copies ran while one was open for 1% -> 1% of each run, Pallas kernels for 0% -> 0%
where the time goes in v1:
time: 502 us; the launch traced here: 498 us
  blocking collectives  209 us (42%)
  waiting for transfers between devices  190 us (38%)
  matrix products  29.4 us (6%)
  local copies, waits for them, and re-layouts  28.9 us (6%)
  between operations  16.2 us (3%)
  loops' own time  13.6 us (3%)
  other arithmetic  10.7 us (2%)
    unnamed x6, waiting for transfers between devices  190 us
    psum x1, blocking collectives, on_device(): depth_whole = lax.psum(depth_sum, ('ia', 'ja'))  120 us
    all_gather x1, blocking collectives, on_device(): row_table = lax.all_gather(factor_rows, ('ja', 'ka'), axis=1, tiled=True)  46.2 us
    all_gather x1, blocking collectives, on_device(): col_table = lax.all_gather(factor_cols, 'ka', axis=1, tiled=True)  24.6 us
    psum x1, blocking collectives, on_device(): cols_whole = lax.psum(cols_sum, 'ia')  18.1 us
    another operation x1, loops' own time, accumulate_blocks(): return lax.fori_loop(0, live_count, add_slot, start_sums)  13.6 us
    dot_general x5, matrix products, block_terms(): lax.dot_general(row_factor, second_flat, (((0,), (0,)), ((), ())), prefer...  13.3 us
    convert_element_type x5, other arithmetic, block_terms(): observed_block.reshape(block_rows, slab_depth * block_cols)  10.7 us
  transfers between devices with their start and end apart: 4, of which 1 were waited for; matrix products, arithmetic and copies ran while one was open for 1% of the time, Pallas kernels for 0%

profile of v1, /device:TPU:2, one launch (start us, length us, event | category | flops | bytes accessed | tf_op | source)
XLA Modules:
  0.0 497.6 jit_solution(12647583901594769200)
XLA Ops:
  8.0 46.2 %all_gather.7 = bf16[64,1024]{0,1:T(8,128)(2,1)S(1)} all-gather(bf16[64,16]{0,1:T(8,128)(2,1)} %param.14), channel_id=1, replica_groups=mesh['ia'=4,'ja'=8,'ka'=8] {'ja','ka'}, dimensions={1}, use_global_device_ids=true | all-gather | bytes 133120 | tf_op jit(solution)/shard_map/all_gather | solution.py:112
  54.3 1.1 copy.25
  55.5 0.8 copy.23
  56.3 24.6 %all_gather.6 = bf16[64,512]{0,1:T(8,128)(2,1)S(1)} all-gather(bf16[64,64]{0,1:T(8,128)(2,1)S(1)} %copy.23), channel_id=1, replica_groups=mesh['ia'=4,'ja'=8,'ka'=8] {'ka'}, dimensions={1}, use_global_device_ids=true | all-gather | bytes 73728 | tf_op jit(solution)/shard_map/all_gather | solution.py:113
  81.0 0.7 copy.56
  81.7 1.6 broadcast_in_dim.7
  83.3 69.4 %while.16 = (s32[]{:T(128)}, f32[64,1024]{1,0:T(8,128)S(1)}, f32[64,512]{1,0:T(8,128)S(1)}, f32[64,1024]{0,1:T(8,128)S(1)}, f32[64,64,64]{2,1,0:T(8,128)}, /*ind...) while((s32[]{:T(128)}, f32[64,1024]{1,0:T(8,128)S(1)}, ...), condition=%wide.region_1.0_spmd, body=%wide.region_0.0_spmd.sunk | while | flops 356534272 | bytes 34849308 | solution.py:101
  84.1 0.6 fusion.87
  85.2 0.4 fusion.88
  85.6 0.6 reshape.62
  86.8 0.4 convolution_convert_fusion.6
  87.9 2.1 dynamic-slice_convert_fusion.3
  90.0 2.7 fusion.89
  93.4 0.9 copy-done.1
  94.3 0.7 convolution_add_fusion.3
  95.3 1.0 copy-done.2
  96.6 0.5 fusion.90
  97.8 0.6 fusion.87
  98.9 0.4 fusion.88
  99.4 0.6 reshape.62
  101.6 2.1 dynamic-slice_convert_fusion.3
  103.8 2.7 fusion.89
  107.1 0.9 copy-done.1
  108.0 0.7 convolution_add_fusion.3
  109.0 1.0 copy-done.2
  110.3 0.5 fusion.90
  111.6 0.6 fusion.87
  112.7 0.4 fusion.88
  113.1 0.6 reshape.62
  115.4 2.1 dynamic-slice_convert_fusion.3
  117.5 2.7 fusion.89
  120.9 0.9 copy-done.1
  121.8 0.7 convolution_add_fusion.3
  122.8 1.0 copy-done.2
  124.1 0.5 fusion.90
  125.3 0.6 fusion.87
  126.4 0.4 fusion.88
  126.9 0.6 reshape.62
  128.1 0.4 convolution_convert_fusion.6
  129.1 2.1 dynamic-slice_convert_fusion.3
  131.2 2.7 fusion.89
  134.6 0.9 copy-done.1
  135.5 0.7 convolution_add_fusion.3
  136.5 1.0 copy-done.2
  137.8 0.5 fusion.90
  139.1 0.6 fusion.87
  140.2 0.4 fusion.88
  140.6 0.6 reshape.62
  142.9 2.1 dynamic-slice_convert_fusion.3
  145.0 2.7 fusion.89
  148.4 0.9 copy-done.1
  149.3 0.7 convolution_add_fusion.3
  150.3 1.0 copy-done.2
  151.6 0.5 fusion.90
  152.7 1.0 copy.28
  153.8 0.8 copy.31
  154.7 0.9 copy.29
  155.7 189.9 %all-reduce.7.cloned.1.call-done = (f32[64,1024]{0,1:T(8,128)}, f32[64,64,64]{2,1,0:T(8,128)}) async-done(((f32[64,1024]{0,1:T(8,128)}, f32[64,64,64]{2,1,0:T(8,128)}), (f32[64,1024]{0,1:T(8,128)}, f32[64,64,64]{2,1,0:T(8,128)})) %all-reduce.7.cloned.1.call-update) | async-done | bytes 1310736
  345.6 0.6 dynamic-slice
  346.9 0.8 copy.32
  347.7 18.1 %psum.32 = f32[64,64]{1,0:T(8,128)} all-reduce(f32[64,64]{1,0:T(8,128)S(1)} %copy.32), channel_id=1, replica_groups=mesh['ia'=4,'ja'=8,'ka'=8] {'ia'}, use_global_device_ids=true, to_apply=%region_3.0 | all-reduce | flops 4096 | bytes 32768 | tf_op jit(solution)/shard_map/psum | solution.py:129
  365.9 119.9 %psum.33 = f32[64,128]{1,0:T(8,128)} all-reduce(f32[64,128]{1,0:T(8,128)} %reduce-scatter.5.cloned.1.call-done), channel_id=1, replica_groups=mesh['ia'=4,'ja'=8,'ka'=8] {'ia','ja'}, use_global_device_ids=true, to_apply=%region_5.0 | all-reduce | flops 8192 | bytes 65536 | tf_op jit(solution)/shard_map/psum | solution.py:130
  485.7 1.3 constant_dynamic-slice_fusion.1
  487.0 3.2 copy.92
  (63 shorter events, 8.7 us)
Async XLA Ops:
  8.0 337.6 %all-reduce.7.cloned.1.call-start = ((), (), s32[]{:S(2)}) async-start(), calls=%async_computation.5 | async-start | bytes 5242880
  54.2 29.1 %copy-start = (bf16[64,64,64]{2,1,0:T(8,128)(2,1)S(1)}, bf16[64,64,64]{2,1,0:T(8,128)(2,1)}, u32[]{:S(2)}) copy-start(bf16[64,64,64]{2,1,0:T(8,128)(2,1)} %param.17) | copy-start | bytes 1572868
  92.7 1.6 copy-start.1
  94.9 1.3 copy-start.2
  106.4 1.6 copy-start.1
  108.7 1.3 copy-start.2
  120.2 1.6 copy-start.1
  122.4 1.3 copy-start.2
  133.9 1.6 copy-start.1
  136.2 1.3 copy-start.2
  147.7 1.6 copy-start.1
  149.9 1.3 copy-start.2
  153.8 191.9 %copy-start.3 = (u32[256]{0:T(256)S(1)}, u32[256]{0:T(256)}, u32[]{:S(2)}) copy-start(u32[256]{0:T(256)} %constant.44) | copy-start | bytes 3076
  153.8 193.1 %reduce-scatter.7.cloned.1.call-start = ((), (), s32[]{:S(2)}) async-start(), calls=%async_computation.4 | async-start | bytes 294912
  154.7 211.2 %reduce-scatter.5.cloned.1.call-start = ((), (), s32[]{:S(2)}) async-start(), calls=%async_computation.3 | async-start | bytes 294912 | tf_op jit(solution)/shard_map/reduce_scatter | solution.py:133
  155.7 331.4 %all-reduce.5.cloned.1.call-start = ((), (), s32[]{:S(2)}) async-start(), calls=%async_computation.2 | async-start | bytes 4194304 | tf_op jit(solution)/shard_map/psum | solution.py:136
Sparse Core Ops, SparseCore 0:
  153.9 191.6 all-reduce.6
  347.9 62.9 all-reduce.4
Sparse Core Ops, SparseCore 1:
  156.7 36.1 reduce-scatter.6
  195.3 36.0 reduce-scatter.4
